TPU v7x, 512 devices: a whole 4x8x8 slice. The times are simulated.
512 devices in a mesh: dp: 8 (over y), seq: 64 (over z, x, core).
Axes of the slice: x: 4, y: 8, z: 8, core: 2. Of those that a mesh axis runs over, the one named last changes fastest.
Arguments:
- mel_frames: bfloat16 [8, 16384, 128], P('dp', 'seq'), may hold values from -16 to 16
- positions: int32 [8, 8192], P('dp', 'seq'), may hold values from 0 to 16383, as said below
- conv_weight: bfloat16 [128, 3, 1280], replicated, may hold values from -0.3125 to 0.3125
- conv_bias: float32 [1280], replicated, may hold values from -3 to 3
- proj_weight: bfloat16 [1280, 2048], P('dp'), may hold values from -0.15625 to 0.15625
- proj_bias: float32 [2048], replicated, may hold values from -3 to 3
- cotangent: bfloat16 [8, 16384, 2048], P('dp', 'seq'), may hold values from -0.032958984 to 0.032958984
Outputs:
- merged: bfloat16 [8, 16384, 2048], P('dp', 'seq')
- grad_weight: float32 [128, 3, 1280], P('seq', None, 'dp')
Inputs may be any that keep to these rules, and one draw needn't show every extreme that they name: Within a recording the 8192 entries are distinct. Block b of the sequence is positions b * 256 to b * 256 + 255; the 128 tokens of one window put at most 4 entries into any one block, and in each recording one block receives exactly 4 from every window.
All inputs are finite; a program needn't handle non-finite values.
Results may differ from a plain program's by a relative error of at most 0.012.
Values may be sent and summed in bfloat16 or wider, within the bound.
A program may use at most 64 MiB of HBM per device.

v0:
```python
import jax
import jax.numpy as jnp
from jax import lax
from jax.sharding import PartitionSpec as P

SQRT_HALF = 0.7071067811865476
INV_SQRT_TWO_PI = 0.3989422804014327


def body(mel_frames, positions, conv_weight, conv_bias, proj_weight, proj_bias, cotangent):
    frames = mel_frames[0]
    spots = positions[0]
    grads_in = cotangent[0]
    n_own = lax.axis_size("seq")
    n_dp = lax.axis_size("dp")
    frame_count, mels = frames.shape
    tok = frame_count // 2
    rows_own, feats = grads_in.shape
    cap = rows_own // n_own
    taps = conv_weight.shape[1]
    ch = conv_weight.shape[2]
    f32, bf16 = (jnp.float32, jnp.bfloat16)
    full_weight = lax.all_gather(proj_weight, "dp", axis=0, tiled=True)
    padded = jnp.pad(frames, ((1, 1), (0, 0)))
    pairs = padded.reshape(tok + 1, 2 * mels)
    windows = jnp.concatenate([pairs[:-1], pairs[1:]], axis=1)
    owner = spots // rows_own
    row = (spots % rows_own).astype(bf16)
    extra = jnp.concatenate([row[:, None] + 1, jnp.zeros((tok, mels - 1), bf16)], axis=1)
    payload = jnp.concatenate([windows, extra], axis=1)
    earlier = jnp.arange(tok)[None, :] < jnp.arange(tok)[:, None]
    rank = jnp.sum((owner[:, None] == owner[None, :]) & earlier, axis=1)
    slot = owner * cap + rank
    place = (jnp.arange(n_own * cap)[:, None] == slot[None, :]).astype(bf16)
    outgoing = jnp.dot(place, payload, preferred_element_type=f32).astype(bf16)
    arrived = lax.all_to_all(
        outgoing.reshape(n_own, cap, -1), "seq", split_axis=0, concat_axis=0, tiled=True
    ).reshape(n_own * cap, -1)
    arrived_row = arrived[:, 4 * mels].astype(jnp.int32) - 1
    pick = jnp.arange(rows_own)[:, None] == arrived_row[None, :]
    used = jnp.any(pick, axis=1)
    x = jnp.dot(pick.astype(bf16), arrived[:, : 4 * mels], preferred_element_type=f32).astype(bf16)
    kernel = jnp.transpose(conv_weight, (1, 0, 2)).reshape(taps * mels, ch)
    x0, x1 = (x[:, : taps * mels], x[:, mels:])
    pre0 = jnp.dot(x0, kernel, preferred_element_type=f32) + conv_bias
    pre1 = jnp.dot(x1, kernel, preferred_element_type=f32) + conv_bias
    phi0 = 0.5 * (1.0 + lax.erf(pre0 * SQRT_HALF))
    phi1 = 0.5 * (1.0 + lax.erf(pre1 * SQRT_HALF))
    pooled = (0.5 * (pre0 * phi0 + pre1 * phi1)).astype(bf16)
    slope0 = phi0 + pre0 * INV_SQRT_TWO_PI * jnp.exp(-0.5 * pre0 * pre0)
    slope1 = phi1 + pre1 * INV_SQRT_TWO_PI * jnp.exp(-0.5 * pre1 * pre1)
    contract_last = (((1,), (1,)), ((), ()))
    grad_pooled = (
        lax.dot_general(grads_in, full_weight, contract_last, preferred_element_type=f32)
        .astype(bf16)
        .astype(f32)
    )
    g0 = (0.5 * grad_pooled * slope0).astype(bf16)
    g1 = (0.5 * grad_pooled * slope1).astype(bf16)
    contract_first = (((0,), (0,)), ((), ()))
    part = lax.dot_general(x0, g0, contract_first, preferred_element_type=f32) + lax.dot_general(
        x1, g1, contract_first, preferred_element_type=f32
    )
    part = part.astype(bf16).reshape(taps, n_own, mels // n_own, ch)
    part = jnp.transpose(part, (1, 2, 0, 3)).reshape(n_own, -1, ch)
    part = lax.all_to_all(part, "seq", split_axis=0, concat_axis=0, tiled=True)
    part = jnp.sum(part.astype(f32), axis=0).astype(bf16)
    part = jnp.transpose(part.reshape(-1, n_dp, ch // n_dp), (1, 0, 2))
    part = lax.all_to_all(part, "dp", split_axis=0, concat_axis=0, tiled=True)
    grad_weight = jnp.sum(part.astype(f32), axis=0).reshape(mels // n_own, taps, ch // n_dp)
    projected = jnp.dot(pooled, full_weight, preferred_element_type=f32) + proj_bias
    merged = jnp.where(used[:, None], projected, 0.0).astype(bf16)
    return (merged[None], grad_weight)


def solution(mesh):
    in_specs = (
        P("dp", "seq", None),
        P("dp", "seq"),
        P(),
        P(),
        P("dp", None),
        P(),
        P("dp", "seq", None),
    )
    out_specs = (P("dp", "seq", None), P("seq", None, "dp"))
    return jax.shard_map(body, mesh=mesh, in_specs=in_specs, out_specs=out_specs, check_vma=False)
```

profile of v0, /device:TPU:2, one launch (start us, length us, event | category | flops | bytes accessed | tf_op | source)
XLA Modules:
  0.0 159.1 jit_solution(6590703125307992225)
XLA Ops:
  7.2 0.7 all-gather.2.cloned.1.call-update
  7.9 0.7 fusion.42
  8.6 0.1 copy.26
  8.7 1.0 pad_slice_fusion.1
  9.8 0.7 fusion.55
  10.5 0.7 and_select_fusion.1
  11.2 0.2 convert_reduce_fusion.1
  11.3 0.7 fusion.44
  12.0 0.2 convolution_convert_fusion.1
  12.4 27.1 %all_to_all.15 = bf16[64,4,640]{2,1,0:T(4,128)(2,1)S(1)} all-to-all(bf16[64,4,640]{2,1,0:T(4,128)(2,1)S(1)} %reshape.128), channel_id=1, replica_groups=mesh['dp'=8,'seq'=64] {'seq'}, dimensions={0} | all-to-all | bytes 655360 | tf_op jit(solution)/shard_map/all_to_all | solution.py:36
  39.5 0.1 add_reduce_fusion
  39.7 0.2 convolution_convert_fusion.2
  39.9 1.8 %convolution_add_fusion.1 = f32[256,1280]{1,0:T(8,128)S(1)} fusion(bf16[384,1280]{1,0:T(8,128)(2,1)} %bitcast.35, f32[1280]{0:T(1024)S(1)} %copy-done.4, bf16[256,512]{1,0:T(8,128)(2,1)S(1)} %convolution_convert_fusion.2), kind=kOutput, calls=%fused_computation.1 | convolution fusion | flops 251985920 | bytes 2498560 | tf_op jit(solution)/shard_map/dot_general | solution.py:46
  41.7 1.6 convolution_add_fusion.2
  43.3 38.4 %all-gather.2.cloned.1.call-done = bf16[1280,2048]{1,0:T(8,128)(2,1)} async-done(((bf16[160,2048]{1,0:T(8,128)(2,1)}), bf16[1280,2048]{1,0:T(8,128)(2,1)}) %all-gather.2.cloned.1.call-update) | async-done | bytes 5242896 | tf_op jit(solution)/shard_map/all_gather | solution.py:23
  81.7 4.2 %fusion.4 = f32[256,1280]{1,0:T(8,128)S(1)} fusion(bf16[1280,2048]{1,0:T(8,128)(2,1)} %all-gather.2.cloned.1.call-done, bf16[1,256,2048]{2,1,0:T(8,128)(2,1)S(1)} %copy-done), kind=kOutput, calls=%fused_computation.9 | convolution fusion | flops 1343160320 | bytes 7602176 | tf_op jit(solution)/shard_map/dot_general | solution.py:54
  85.9 0.8 fusion.18
  86.7 1.8 %fusion = bf16[384,1280]{1,0:T(8,128)(2,1)} fusion(f32[384,1280]{1,0:T(8,128)S(1)} %fusion.18, f32[256,1280]{1,0:T(8,128)S(1)} %fusion.4, f32[256,1280]{1,0:T(8,128)S(1)} %convolution_add_fusion.1, bf16[256,512]{1,0:T(8,128)(2,1)S(1)} %convolution_convert_fusion.2), kind=kOutput, calls=%fused_computation.3 | convolution fusion | flops 255918080 | bytes 5767168 | tf_op jit(solution)/shard_map/dot_general | solution.py:61
  88.6 2.4 %reshape.131 = bf16[3,64,2,1280]{3,2,1,0:T(2,128)(2,1)S(1)} reshape(bf16[384,1280]{1,0:T(8,128)(2,1)} %fusion) | data formatting | bytes 1966080 | tf_op jit(solution)/shard_map/reshape | solution.py:64
  91.0 0.1 copy.27
  91.1 1.7 %copy.28 = bf16[64,6,1280]{2,1,0:T(8,128)(2,1)} copy(bf16[64,6,1280]{2,0,1:T(8,128)(2,1)S(1)} %bitcast.37) | data formatting | bytes 1966080 | tf_op jit(solution)/shard_map/reshape | solution.py:65
  92.8 10.9 %all-to-all-start.1 = ((bf16[64,6,1280]{2,1,0:T(8,128)(2,1)}), bf16[64,6,1280]{2,1,0:T(8,128)(2,1)S(1)}, u32[]{:S(2)}, u32[]{:S(2)}) async-start(bf16[64,6,1280]{2,1,0:T(8,128)(2,1)} %copy.28), calls=%async_computation.1 | async-start | bytes 2621440 | tf_op jit(solution)/shard_map/all_to_all | solution.py:66
  103.7 0.1 fusion.26
  103.9 34.3 %all-to-all-done.1 = bf16[64,6,1280]{2,1,0:T(8,128)(2,1)S(1)} async-done(((bf16[64,6,1280]{2,1,0:T(8,128)(2,1)}), bf16[64,6,1280]{2,1,0:T(8,128)(2,1)S(1)}, u32[]{:S(2)}, u32[]{:S(2)}) %all-to-all-start.1) | async-done | bytes 983072 | tf_op jit(solution)/shard_map/all_to_all | solution.py:66
  138.1 0.3 reduce_sum.34
  138.4 0.1 reshape.133
  138.5 0.7 reshape.136
  139.2 4.5 %all-to-all-start.2 = ((bf16[8,2,480]{2,1,0:T(2,128)(2,1)}), bf16[8,2,480]{2,1,0:T(2,128)(2,1)S(1)}, u32[]{:S(2)}, u32[]{:S(2)}) async-start(bf16[8,2,480]{2,1,0:T(2,128)(2,1)} %reshape.136), calls=%async_computation.2 | async-start | bytes 32768 | tf_op jit(solution)/shard_map/all_to_all | solution.py:69
  143.7 6.1 %fusion.5 = bf16[1,256,2048]{2,1,0:T(8,128)(2,1)} fusion(bf16[1280,2048]{1,0:T(8,128)(2,1)} %all-gather.2.cloned.1.call-done, f32[2048]{0:T(1024)S(1)} %copy-done.5, pred[256]{0:T(512)(128)(4,1)S(1)} %fusion.26, f32[256,1280]{1,0:T(8,128)} %copy-done.1, f32[256,1280]{1,0:T(8,128)} %convolution_add_fusion.2), kind=kOutput, calls=%fused_computation.10 | convolution fusion | flops 1347354624 | bytes 8921344 | tf_op jit(solution)/shard_map/dot_general | solution.py:71
  149.8 1.7 %all-to-all-done.2 = bf16[8,2,480]{2,1,0:T(2,128)(2,1)S(1)} async-done(((bf16[8,2,480]{2,1,0:T(2,128)(2,1)}), bf16[8,2,480]{2,1,0:T(2,128)(2,1)S(1)}, u32[]{:S(2)}, u32[]{:S(2)}) %all-to-all-start.2) | async-done | bytes 15392 | tf_op jit(solution)/shard_map/all_to_all | solution.py:69
  151.5 0.1 reshape.137
  151.6 0.6 copy.30
  (22 shorter events, 0.4 us)
Async XLA Ops:
  7.2 74.6 %copy-start = (bf16[1,256,2048]{2,1,0:T(8,128)(2,1)S(1)}, bf16[1,256,2048]{2,1,0:T(8,128)(2,1)}, u32[]{:S(2)}) copy-start(bf16[1,256,2048]{2,1,0:T(8,128)(2,1)} %param.13) | copy-start | bytes 3145732
  7.2 74.5 %all-gather.2.cloned.1.call-start = ((), (), s32[]{:S(2)}) async-start(), calls=%async_computation.3 | async-start | bytes 5898240 | tf_op jit(solution)/shard_map/all_gather | solution.py:23
  12.3 27.6 %copy-start.4 = (f32[1280]{0:T(1024)S(1)}, f32[1280]{0:T(1024)}, u32[]{:S(2)}) copy-start(f32[1280]{0:T(1024)} %param.10) | copy-start | bytes 15364
  39.9 1.8 %copy-start.3 = (bf16[128,3,1280]{2,0,1:T(8,128)(2,1)S(1)}, bf16[128,3,1280]{2,0,1:T(8,128)(2,1)}, u32[]{:S(2)}) copy-start(bf16[128,3,1280]{2,0,1:T(8,128)(2,1)} %param.9) | copy-start | bytes 2949124
  41.7 45.0 %copy-start.1 = (f32[256,1280]{1,0:T(8,128)}, f32[256,1280]{1,0:T(8,128)S(1)}, u32[]{:S(2)}) copy-start(f32[256,1280]{1,0:T(8,128)S(1)} %convolution_add_fusion.1) | copy-start | bytes 3932164
  81.7 4.2 %copy-start.2 = (f32[256,1280]{1,0:T(8,128)S(1)}, f32[256,1280]{1,0:T(8,128)}, u32[]{:S(2)}) copy-start(f32[256,1280]{1,0:T(8,128)} %convolution_add_fusion.2) | copy-start | bytes 3932164
  92.8 45.3 %all-to-all-start.1 = ((bf16[64,6,1280]{2,1,0:T(8,128)(2,1)}), bf16[64,6,1280]{2,1,0:T(8,128)(2,1)S(1)}, u32[]{:S(2)}, u32[]{:S(2)}) async-start(bf16[64,6,1280]{2,1,0:T(8,128)(2,1)} %copy.28), calls=%async_computation.1 | async-start | bytes 2621440 | tf_op jit(solution)/shard_map/all_to_all | solution.py:66
  103.7 40.0 %copy-start.5 = (f32[2048]{0:T(1024)S(1)}, f32[2048]{0:T(1024)}, u32[]{:S(2)}) copy-start(f32[2048]{0:T(1024)} %param.12) | copy-start | bytes 24580
  139.2 12.2 %all-to-all-start.2 = ((bf16[8,2,480]{2,1,0:T(2,128)(2,1)}), bf16[8,2,480]{2,1,0:T(2,128)(2,1)S(1)}, u32[]{:S(2)}, u32[]{:S(2)}) async-start(bf16[8,2,480]{2,1,0:T(2,128)(2,1)} %reshape.136), calls=%async_computation.2 | async-start | bytes 32768 | tf_op jit(solution)/shard_map/all_to_all | solution.py:69
Sparse Core Ops, SparseCore 0:
  10.1 71.5 all-gather.1
where the time goes:
time: 160 us; the launch traced here: 159 us
  waiting for transfers between devices  75.1 us (47%)
  blocking collectives  27.1 us (17%)
  matrix products  16.7 us (10%)
  starting transfers between devices  15.4 us (10%)
  between operations  14.2 us (9%)
  local copies, waits for them, and re-layouts  7.17 us (4%)
  other arithmetic  3.37 us (2%)
    all_gather x1, waiting for transfers between devices, body(): full_weight = lax.all_gather(proj_weight, 'dp', axis=0, tiled=True)  38.4 us
    all_to_all x1, waiting for transfers between devices, body(): part = lax.all_to_all(part, 'seq', split_axis=0, concat_axis=0, tiled=True)  34.3 us
    all_to_all x1, blocking collectives, body(): lax.all_to_all(outgoing.reshape(n_own, cap, -1), 'seq', split_axis=0, con...  27.1 us
    all_to_all x1, starting transfers between devices, body(): part = lax.all_to_all(part, 'seq', split_axis=0, concat_axis=0, tiled=True)  10.9 us
    dot_general x1, matrix products, body(): jnp.dot(pooled, full_weight, preferred_element_type=f32) + proj_bias  6.07 us
    all_to_all x1, starting transfers between devices, body(): part = lax.all_to_all(part, 'dp', split_axis=0, concat_axis=0, tiled=True)  4.46 us
    dot_general x1, matrix products, body(): lax.dot_general(grads_in, full_weight, contract_last, preferred_element_t...  4.15 us
  transfers between devices with their start and end apart: 3, of which 3 were waited for; matrix products, arithmetic and copies ran while one was open for 9% of the time, Pallas kernels for 0%

commit v1 on v0

--- a/solution.py
+++ b/solution.py
@@ -20,7 +20,11 @@
     taps = conv_weight.shape[1]
     ch = conv_weight.shape[2]
     f32, bf16 = (jnp.float32, jnp.bfloat16)
-    full_weight = lax.all_gather(proj_weight, "dp", axis=0, tiled=True)
+    produce_entries = lambda a0: jnp.concatenate(
+        lax.all_to_all(jnp.stack([a0 for _ in range(lax.psum(1, "dp"))], axis=0), "dp", 0, 0),
+        axis=0,
+    )
+    full_weight = produce_entries(proj_weight)
     padded = jnp.pad(frames, ((1, 1), (0, 0)))
     pairs = padded.reshape(tok + 1, 2 * mels)
     windows = jnp.concatenate([pairs[:-1], pairs[1:]], axis=1)

time: 160 us -> 226 us (1.41)
  waiting for transfers between devices: 75.1 us -> 151 us
  between operations: 14.2 us -> 0.84 us
  local copies, waits for them, and re-layouts: 7.17 us -> 10.1 us
    all_to_all x0 -> x1, waiting for transfers between devices: none -> 115 us  [body(): lax.all_to_all(jnp.stack([a0 for _ in range(lax.psum(1, 'dp'))], axis=0),...]
    all_gather x1 -> x0, waiting for transfers between devices: 38.4 us -> none  [body(): full_weight = lax.all_gather(proj_weight, 'dp', axis=0, tiled=True)]
    all_to_all x0 -> x1, starting transfers between devices: none -> 7.23 us  [body(): lax.all_to_all(jnp.stack([a0 for _ in range(lax.psum(1, 'dp'))], axis=0),...]
    all_to_all x1, starting transfers between devices: 10.9 us -> 5.51 us  [body(): part = lax.all_to_all(part, 'seq', split_axis=0, concat_axis=0, tiled=True)]
    another operation x0 -> x1, local copies, waits for them, and re-layouts: none -> 3.01 us  [body(): jnp.stack([a0 for _ in range(lax.psum(1, 'dp'))], axis=0)]
  transfers between devices with their start and end apart: 3 -> 3, of which waited for: 3 -> 3; matrix products, arithmetic and copies ran while one was open for 9% -> 4% of each run, Pallas kernels for 0% -> 0%
where the time goes in v1:
time: 226 us
  waiting for transfers between devices  151 us (67%)
  blocking collectives  27.1 us (12%)
  matrix products  16.7 us (7%)
  starting transfers between devices  16.1 us (7%)
  local copies, waits for them, and re-layouts  10.1 us (4%)
  other arithmetic  3.49 us (2%)
    all_to_all x1, waiting for transfers between devices, body(): lax.all_to_all(jnp.stack([a0 for _ in range(lax.psum(1, 'dp'))], axis=0),...  115 us
    all_to_all x1, waiting for transfers between devices, body(): part = lax.all_to_all(part, 'seq', split_axis=0, concat_axis=0, tiled=True)  34.3 us
    all_to_all x1, blocking collectives, body(): lax.all_to_all(outgoing.reshape(n_own, cap, -1), 'seq', split_axis=0, con...  27.1 us
    all_to_all x1, starting transfers between devices, body(): lax.all_to_all(jnp.stack([a0 for _ in range(lax.psum(1, 'dp'))], axis=0),...  7.23 us
    dot_general x1, matrix products, body(): jnp.dot(pooled, full_weight, preferred_element_type=f32) + proj_bias  6.07 us
    all_to_all x1, starting transfers between devices, body(): part = lax.all_to_all(part, 'seq', split_axis=0, concat_axis=0, tiled=True)  5.51 us
  transfers between devices with their start and end apart: 3, of which 3 were waited for; matrix products, arithmetic and copies ran while one was open for 4% of the time, Pallas kernels for 0%

profile of v1, /device:TPU:2, one launch (start us, length us, event | category | flops | bytes accessed | tf_op | source)
XLA Modules:
  0.0 225.7 jit_solution(6448487089758118575)
XLA Ops:
  0.7 0.8 fusion.42
  1.4 0.7 fusion.55
  2.1 0.7 and_select_fusion.1
  2.8 0.1 copy.26
  2.9 1.0 pad_slice_fusion.1
  3.9 0.2 convert_reduce_fusion.1
  4.1 0.7 fusion.44
  4.9 0.2 convolution_convert_fusion.1
  5.2 27.1 %all_to_all.20 = bf16[64,4,640]{2,1,0:T(4,128)(2,1)S(1)} all-to-all(bf16[64,4,640]{2,1,0:T(4,128)(2,1)S(1)} %reshape.133), channel_id=1, replica_groups=mesh['dp'=8,'seq'=64] {'seq'}, dimensions={0} | all-to-all | bytes 655360 | tf_op jit(solution)/shard_map/all_to_all | solution.py:40
  32.3 3.0 %stack.2 = bf16[8,160,2048]{2,1,0:T(8,128)(2,1)} broadcast(bf16[160,2048]{1,0:T(8,128)(2,1)S(1)} %copy-done.4), dimensions={1,2} | broadcast | bytes 5898240 | tf_op jit(solution)/shard_map/stack | solution.py:24
  35.3 7.2 %all-to-all-start.1 = ((bf16[8,160,2048]{2,1,0:T(8,128)(2,1)}), bf16[8,160,2048]{2,1,0:T(8,128)(2,1)}, u32[]{:S(2)}, u32[]{:S(2)}) async-start(bf16[8,160,2048]{2,1,0:T(8,128)(2,1)} %stack.2), calls=%async_computation.1 | async-start | bytes 10485760 | tf_op jit(solution)/shard_map/all_to_all | solution.py:24
  42.6 0.1 add_reduce_fusion
  42.8 0.2 convolution_convert_fusion.2
  43.0 1.8 convolution_add_fusion.1
  44.8 1.6 convolution_add_fusion.2
  46.4 115.4 %all-to-all-done.1 = bf16[8,160,2048]{2,1,0:T(8,128)(2,1)} async-done(((bf16[8,160,2048]{2,1,0:T(8,128)(2,1)}), bf16[8,160,2048]{2,1,0:T(8,128)(2,1)}, u32[]{:S(2)}, u32[]{:S(2)}) %all-to-all-start.1) | async-done | bytes 5242912 | tf_op jit(solution)/shard_map/all_to_all | solution.py:24
  161.9 4.1 %fusion.4 = f32[256,1280]{1,0:T(8,128)S(1)} fusion(bf16[1280,2048]{1,0:T(8,128)(2,1)} %bitcast.9, bf16[1,256,2048]{2,1,0:T(8,128)(2,1)S(1)} %copy-done), kind=kOutput, calls=%fused_computation.9 | convolution fusion | flops 1343160320 | bytes 7602176 | tf_op jit(solution)/shard_map/dot_general | solution.py:58
  166.0 0.8 fusion.18
  166.9 1.8 fusion
  168.7 2.4 %reshape.137 = bf16[3,64,2,1280]{3,2,1,0:T(2,128)(2,1)S(1)} reshape(bf16[384,1280]{1,0:T(8,128)(2,1)} %fusion) | data formatting | bytes 1966080 | tf_op jit(solution)/shard_map/reshape | solution.py:68
  171.2 1.7 copy.28
  172.9 5.5 %all-to-all-start.2 = ((bf16[64,6,1280]{2,1,0:T(8,128)(2,1)}), bf16[64,6,1280]{2,1,0:T(8,128)(2,1)S(1)}, u32[]{:S(2)}, u32[]{:S(2)}) async-start(bf16[64,6,1280]{2,1,0:T(8,128)(2,1)} %copy.28), calls=%async_computation.2 | async-start | bytes 2621440 | tf_op jit(solution)/shard_map/all_to_all | solution.py:70
  178.4 0.1 fusion.26
  178.5 34.3 %all-to-all-done.2 = bf16[64,6,1280]{2,1,0:T(8,128)(2,1)S(1)} async-done(((bf16[64,6,1280]{2,1,0:T(8,128)(2,1)}), bf16[64,6,1280]{2,1,0:T(8,128)(2,1)S(1)}, u32[]{:S(2)}, u32[]{:S(2)}) %all-to-all-start.2) | async-done | bytes 983072 | tf_op jit(solution)/shard_map/all_to_all | solution.py:70
  212.8 0.3 reduce_sum.34
  213.1 0.1 reshape.139
  213.2 0.7 reshape.142
  213.9 3.3 %all-to-all-start.3 = ((bf16[8,2,480]{2,1,0:T(2,128)(2,1)}), bf16[8,2,480]{2,1,0:T(2,128)(2,1)S(1)}, u32[]{:S(2)}, u32[]{:S(2)}) async-start(bf16[8,2,480]{2,1,0:T(2,128)(2,1)} %reshape.142), calls=%async_computation.3 | async-start | bytes 32768 | tf_op jit(solution)/shard_map/all_to_all | solution.py:73
  217.2 6.1 %fusion.5 = bf16[1,256,2048]{2,1,0:T(8,128)(2,1)} fusion(bf16[1280,2048]{1,0:T(8,128)(2,1)} %bitcast.9, f32[2048]{0:T(1024)S(1)} %copy-done.6, pred[256]{0:T(512)(128)(4,1)S(1)} %fusion.26, f32[256,1280]{1,0:T(8,128)} %copy-done.1, f32[256,1280]{1,0:T(8,128)} %convolution_add_fusion.2), kind=kOutput, calls=%fused_computation.10 | convolution fusion | flops 1347354624 | bytes 8921344 | tf_op jit(solution)/shard_map/dot_general | solution.py:75
  223.3 1.6 all-to-all-done.3
  224.9 0.1 reshape.143
  225.1 0.6 copy.30
  (24 shorter events, 0.5 us)
Async XLA Ops:
  0.6 161.2 %copy-start = (bf16[1,256,2048]{2,1,0:T(8,128)(2,1)S(1)}, bf16[1,256,2048]{2,1,0:T(8,128)(2,1)}, u32[]{:S(2)}) copy-start(bf16[1,256,2048]{2,1,0:T(8,128)(2,1)} %param.13) | copy-start | bytes 3145732
  0.6 31.7 %copy-start.4 = (bf16[160,2048]{1,0:T(8,128)(2,1)S(1)}, bf16[160,2048]{1,0:T(8,128)(2,1)}, u32[]{:S(2)}) copy-start(bf16[160,2048]{1,0:T(8,128)(2,1)} %param.11) | copy-start | bytes 1966084
  35.3 7.7 %copy-start.5 = (f32[1280]{0:T(1024)S(1)}, f32[1280]{0:T(1024)}, u32[]{:S(2)}) copy-start(f32[1280]{0:T(1024)} %param.10) | copy-start | bytes 15364
  35.3 126.5 %all-to-all-start.1 = ((bf16[8,160,2048]{2,1,0:T(8,128)(2,1)}), bf16[8,160,2048]{2,1,0:T(8,128)(2,1)}, u32[]{:S(2)}, u32[]{:S(2)}) async-start(bf16[8,160,2048]{2,1,0:T(8,128)(2,1)} %stack.2), calls=%async_computation.1 | async-start | bytes 10485760 | tf_op jit(solution)/shard_map/all_to_all | solution.py:24
  43.0 1.8 copy-start.3
  44.8 122.0 %copy-start.1 = (f32[256,1280]{1,0:T(8,128)}, f32[256,1280]{1,0:T(8,128)S(1)}, u32[]{:S(2)}) copy-start(f32[256,1280]{1,0:T(8,128)S(1)} %convolution_add_fusion.1) | copy-start | bytes 3932164
  161.9 4.2 %copy-start.2 = (f32[256,1280]{1,0:T(8,128)S(1)}, f32[256,1280]{1,0:T(8,128)}, u32[]{:S(2)}) copy-start(f32[256,1280]{1,0:T(8,128)} %convolution_add_fusion.2) | copy-start | bytes 3932164
  172.9 39.9 %all-to-all-start.2 = ((bf16[64,6,1280]{2,1,0:T(8,128)(2,1)}), bf16[64,6,1280]{2,1,0:T(8,128)(2,1)S(1)}, u32[]{:S(2)}, u32[]{:S(2)}) async-start(bf16[64,6,1280]{2,1,0:T(8,128)(2,1)} %copy.28), calls=%async_computation.2 | async-start | bytes 2621440 | tf_op jit(solution)/shard_map/all_to_all | solution.py:70
  178.4 38.9 %copy-start.6 = (f32[2048]{0:T(1024)S(1)}, f32[2048]{0:T(1024)}, u32[]{:S(2)}) copy-start(f32[2048]{0:T(1024)} %param.12) | copy-start | bytes 24580
  213.9 11.0 %all-to-all-start.3 = ((bf16[8,2,480]{2,1,0:T(2,128)(2,1)}), bf16[8,2,480]{2,1,0:T(2,128)(2,1)S(1)}, u32[]{:S(2)}, u32[]{:S(2)}) async-start(bf16[8,2,480]{2,1,0:T(2,128)(2,1)} %reshape.142), calls=%async_computation.3 | async-start | bytes 32768 | tf_op jit(solution)/shard_map/all_to_all | solution.py:73
